TPU v7x, 32 devices: a whole 2x2x4 slice. The times are simulated.
32 devices in a mesh: ctx: 8 (over z, x), head: 4 (over y, core).
Axes of the slice: x: 2, y: 2, z: 4, core: 2. Of those that a mesh axis runs over, the one named last changes fastest.
Arguments:
- keys: bfloat16 [16384, 5120], P('ctx', 'head'), may hold values from -6 to 6
- values: bfloat16 [16384, 5120], P('ctx', 'head'), may hold values from -6 to 6
- queries: bfloat16 [16384, 5120], P('ctx', 'head'), may hold values from -6 to 6
- rates: float32 [16384, 16], P('ctx', 'head'), may hold values from 9.765625e-05 to 0.0009765625
- w_gate: bfloat16 [320, 16, 320], P('ctx', 'head'), may hold values from -0.3125 to 0.3125
- w_up: bfloat16 [320, 16, 320], P('ctx', 'head'), may hold values from -0.3125 to 0.3125
- w_down: bfloat16 [320, 16, 320], P('ctx', 'head'), may hold values from -0.3125 to 0.3125
- gain: float32 [5120], P('head'), may hold values from 0.5 to 1.5
Outputs:
- output: bfloat16 [16384, 5120], P('ctx', 'head')
- new_gate: bfloat16 [320, 16, 320], P('ctx', 'head')
- new_up: bfloat16 [320, 16, 320], P('ctx', 'head')
- new_down: bfloat16 [320, 16, 320], P('ctx', 'head')
All inputs are finite; a program needn't handle non-finite values.
Results may differ from a plain program's by a relative error of at most 0.0092.
Values may be sent and summed in bfloat16 or wider, within the bound.
A program may use at most 128 MiB of HBM per device.

v0:
```python
import jax
import jax.numpy as jnp
from jax import lax
from jax.sharding import PartitionSpec as P

HEADS = 16
DH = 320


EPS = 1e-06


def per_device(keys, values, queries, rates, w_gate, w_up, w_down, gain):
    rows = keys.shape[0]
    heads = w_gate.shape[1]
    width = w_gate.shape[2]
    local_units = w_gate.shape[0]
    keyh = keys.reshape(rows, heads, width)
    valueh = values.reshape(rows, heads, width)
    queryh = queries.reshape(rows, heads, width)
    full_gate, full_up, full_down = (
        lax.all_gather(w_gate, "ctx", axis=0, tiled=True),
        lax.all_gather(w_up, "ctx", axis=0, tiled=True),
        lax.all_gather(w_down, "ctx", axis=0, tiled=True),
    )
    gpre = jnp.einsum("thd,fhd->thf", keyh, full_gate, preferred_element_type=jnp.float32)
    upre = jnp.einsum("thd,fhd->thf", keyh, full_up, preferred_element_type=jnp.float32)
    sig = jax.nn.sigmoid(gpre)
    act = gpre * sig
    slope = sig * (1.0 + gpre * (1.0 - sig))
    hidden = (act * upre).astype(jnp.bfloat16)
    scaled = (valueh.astype(jnp.float32) * rates[:, :, None]).astype(jnp.bfloat16)
    back = jnp.einsum("thd,fhd->thf", scaled, full_down, preferred_element_type=jnp.float32)
    dgate = (back * upre * slope).astype(jnp.bfloat16)
    dup = (back * act).astype(jnp.bfloat16)
    grad_gate = jnp.einsum("thf,thd->fhd", dgate, keyh, preferred_element_type=jnp.float32)
    grad_up = jnp.einsum("thf,thd->fhd", dup, keyh, preferred_element_type=jnp.float32)
    grad_down = jnp.einsum("thf,thd->fhd", hidden, scaled, preferred_element_type=jnp.float32)
    total = lax.psum(jnp.stack([grad_gate, grad_up, grad_down], axis=1), "ctx")
    olds = jnp.stack([full_gate, full_up, full_down], axis=1).astype(jnp.float32)
    updated = olds + total
    old_sq = jnp.sum(olds * olds, axis=0)
    new_sq = jnp.sum(updated * updated, axis=0)
    fresh = (updated * (jnp.sqrt(old_sq) * lax.rsqrt(new_sq + EPS))[None]).astype(jnp.bfloat16)
    offset = lax.axis_index("ctx") * local_units
    mine = lax.dynamic_slice_in_dim(fresh, offset, local_units, 0)
    new_gate = fresh[:, 0]
    new_up = fresh[:, 1]
    new_down = fresh[:, 2]
    qgate = jnp.einsum("thd,fhd->thf", queryh, new_gate, preferred_element_type=jnp.float32)
    qup = jnp.einsum("thd,fhd->thf", queryh, new_up, preferred_element_type=jnp.float32)
    mixed = (jax.nn.silu(qgate) * qup).astype(jnp.bfloat16)
    outh = jnp.einsum("thf,fhd->thd", mixed, new_down, preferred_element_type=jnp.float32)
    squares = lax.psum(jnp.sum(outh * outh, axis=(1, 2)), "head")
    scale = lax.rsqrt(squares / (HEADS * DH) + EPS)
    result = outh * scale[:, None, None] * gain.reshape(heads, width)[None]
    output = result.reshape(rows, heads * width).astype(jnp.bfloat16)
    return (output, mine[:, 0], mine[:, 1], mine[:, 2])


def solution(mesh):
    in_specs = (
        P("ctx", "head"),
        P("ctx", "head"),
        P("ctx", "head"),
        P("ctx", "head"),
        P("ctx", "head", None),
        P("ctx", "head", None),
        P("ctx", "head", None),
        P("head"),
    )
    out_specs = (
        P("ctx", "head"),
        P("ctx", "head", None),
        P("ctx", "head", None),
        P("ctx", "head", None),
    )
    return jax.shard_map(
        per_device, mesh=mesh, in_specs=in_specs, out_specs=out_specs, check_vma=False
    )
```

profile of v0, /device:TPU:22, one launch (start us, length us, event | category | flops | bytes accessed | tf_op | source)
XLA Modules:
  0.0 444.0 jit_solution(6353832946601583923)
XLA Ops:
  7.2 0.0 copy-start.5
  7.2 0.0 copy-start.6
  7.2 0.0 all-reduce.2.cloned.1.call-start
  7.2 7.9 %copy.31 = bf16[2048,1280]{0,1:T(8,128)(2,1)} copy(bf16[2048,1280]{1,0:T(8,128)(2,1)} %param.8) | data formatting | bytes 10485760 | tf_op args[0]
  15.2 0.0 copy-done.5
  15.2 31.1 %all_gather.9 = bf16[320,4,320]{2,0,1:T(8,128)(2,1)S(1)} all-gather(bf16[40,4,320]{2,0,1:T(8,128)(2,1)S(1)} %copy.27), channel_id=1, replica_groups=mesh['ctx'=8,'head'=4] {'ctx'}, dimensions={0}, use_global_device_ids=true | all-gather | bytes 921600 | tf_op jit(solution)/shard_map/all_gather | solution.py:22
  46.3 0.0 copy-done.6
  46.3 0.0 slice-start
  46.3 33.4 %all_gather.10 = bf16[320,4,320]{2,0,1:T(8,128)(2,1)S(1)} all-gather(bf16[40,4,320]{2,0,1:T(8,128)(2,1)S(1)} %copy.28), channel_id=1, replica_groups=mesh['ctx'=8,'head'=4] {'ctx'}, dimensions={0}, use_global_device_ids=true | all-gather | bytes 921600 | tf_op jit(solution)/shard_map/all_gather | solution.py:23
  79.7 0.0 slice-start.1
  79.7 8.1 %fusion.45 = f32[4,320,2048]{2,1,0:T(8,128)} fusion(bf16[320,4,320]{2,0,1:T(8,128)(2,1)S(1)} %all_gather.9, bf16[2048,4,320]{0,2,1:T(8,128)(2,1)} %bitcast.133), kind=kOutput, calls=%fused_computation.56 | convolution fusion | flops 1677721600 | bytes 16547840 | tf_op jit(solution)/shard_map/thd,fhd->thf/dot_general | solution.py:26
  87.8 0.0 slice-done
  87.8 0.0 slice-done.1
  87.8 5.4 %fusion.44 = f32[4,320,2048]{2,1,0:T(8,128)} fusion(bf16[320,4,320]{2,0,1:T(8,128)(2,1)S(1)} %all_gather.10, bf16[2048,4,320]{0,2,1:T(8,128)(2,1)S(1)} %bitcast.138), kind=kOutput, calls=%fused_computation.55 | convolution fusion | flops 1677721600 | bytes 16547840 | tf_op jit(solution)/shard_map/thd,fhd->thf/dot_general | solution.py:27
  93.2 0.0 copy-start.7
  93.2 8.0 %copy.30 = bf16[2048,1280]{0,1:T(8,128)(2,1)} copy(bf16[2048,1280]{1,0:T(8,128)(2,1)} %param.9) | data formatting | bytes 10485760 | tf_op args[1]
  101.2 0.0 copy-done.7
  101.2 32.6 %all_gather.11 = bf16[320,4,320]{2,0,1:T(8,128)(2,1)S(1)} all-gather(bf16[40,4,320]{2,0,1:T(8,128)(2,1)S(1)} %copy.29), channel_id=1, replica_groups=mesh['ctx'=8,'head'=4] {'ctx'}, dimensions={0}, use_global_device_ids=true | all-gather | bytes 921600 | tf_op jit(solution)/shard_map/all_gather | solution.py:24
  133.8 0.0 copy-done.4
  133.8 7.9 %fusion.24 = f32[4,2048,320]{1,2,0:T(8,128)} fusion(bf16[320,4,320]{2,0,1:T(8,128)(2,1)S(1)} %all_gather.11, bf16[2048,4,320]{0,2,1:T(8,128)(2,1)} %bitcast.143, f32[2048,4]{0,1:T(4,128)S(1)} %copy-done.4), kind=kOutput, calls=%fused_computation.36 | convolution fusion | flops 1685585920 | bytes 16580608 | tf_op jit(solution)/shard_map/thd,fhd->thf/dot_general | solution.py:33
  141.7 13.0 %fusion.31 = f32[320,1,4,320]{3,0,2,1:T(8,128)} fusion(f32[4,320,2048]{2,1,0:T(8,128)} %fusion.44, f32[4,320,2048]{2,1,0:T(8,128)} %fusion.45, bf16[2048,4,320]{0,2,1:T(8,128)(2,1)} %bitcast.144, f32[2048,4]{0,1:T(4,128)S(1)} %copy-done.4), kind=kOutput, calls=%fused_computation.40 | convolution fusion | flops 1701314560 | bytes 27885568 | tf_op jit(solution)/shard_map/thf,thd->fhd/dot_general | solution.py:38
  154.7 15.3 %fusion.28 = f32[320,1,4,320]{3,0,2,1:T(8,128)} fusion(bf16[2048,4,320]{0,2,1:T(8,128)(2,1)} %bitcast.134, f32[4,320,2048]{2,1,0:T(8,128)} %fusion.45, f32[4,320,2048]{2,1,0:T(8,128)} %fusion.44, f32[4,2048,320]{1,2,0:T(8,128)} %fusion.24), kind=kOutput, calls=%fused_computation.39 | convolution fusion | flops 1703936000 | bytes 38338560 | tf_op jit(solution)/shard_map/thf,thd->fhd/dot_general | solution.py:36
  170.0 10.7 %fusion.36 = f32[320,1,4,320]{3,0,2,1:T(8,128)S(1)} fusion(bf16[2048,4,320]{0,2,1:T(8,128)(2,1)} %bitcast.135, f32[4,2048,320]{1,2,0:T(8,128)} %fusion.24, f32[4,320,2048]{2,1,0:T(8,128)} %fusion.45), kind=kOutput, calls=%fused_computation.41 | convolution fusion | flops 1693450240 | bytes 27852800 | tf_op jit(solution)/shard_map/thf,thd->fhd/dot_general | solution.py:37
  180.7 0.0 copy-done.2
  180.8 0.0 copy-done.3
  180.8 3.0 pad_maximum_fusion
  183.8 0.0 all-reduce.2.cloned.1.call-update
  183.8 0.0 copy-start.8
  183.8 7.9 %copy.33 = bf16[2048,1280]{0,1:T(8,128)(2,1)} copy(bf16[2048,1280]{1,0:T(8,128)(2,1)} %param.10) | data formatting | bytes 10485760 | tf_op args[2]
  191.7 0.0 copy-done.8
  191.7 0.1 mul.103
  191.8 194.9 %all-reduce.2.cloned.1.call-done = f32[320,3,4,320]{3,0,2,1:T(8,128)} async-done(((f32[320,3,4,320]{3,0,2,1:T(8,128)}), f32[320,3,4,320]{3,0,2,1:T(8,128)}) %all-reduce.2.cloned.1.call-update) | async-done | bytes 4915216 | tf_op jit(solution)/shard_map/psum | solution.py:39
  386.6 3.6 fusion.14
  390.3 0.8 copy-done
  391.0 1.0 multiply_convert_fusion.1
  392.1 0.0 copy-start.1
  392.1 1.6 copy-done.1
  393.7 0.0 slice-done.2
  393.7 0.0 slice-done.3
  393.7 5.4 %fusion.39 = f32[4,320,2048]{2,1,0:T(8,128)} fusion(bf16[2048,4,320]{0,2,1:T(8,128)(2,1)S(1)} %bitcast.142, bf16[320,3,4,320]{3,0,2,1:T(8,128)(2,1)S(1)} %multiply_convert_fusion.1), kind=kOutput, calls=%fused_computation.44 | convolution fusion | flops 1677721600 | bytes 16711680 | tf_op jit(solution)/shard_map/thd,fhd->thf/dot_general | solution.py:50
  399.1 13.7 %multiply_reduce_fusion = (f32[2048]{0:T(1024)S(1)}, f32[4,320,2048]{2,1,0:T(8,128)}) fusion(f32[4,320,2048]{2,1,0:T(8,128)} %fusion.39, bf16[2048,4,320]{0,2,1:T(8,128)(2,1)} %bitcast.139, bf16[320,3,4,320]{3,0,2,1:T(8,128)(2,1)} %copy-done.1), kind=kOutput, calls=%fused_computation.25 | convolution fusion | flops 3376412672 | bytes 28188672 | tf_op jit(solution)/shard_map/thf,fhd->thd/dot_general | solution.py:53
  412.8 6.1 %psum.15 = f32[2048]{0:T(1024)S(1)} all-reduce(f32[2048]{0:T(1024)S(1)} %get-tuple-element.17), channel_id=1, replica_groups=mesh['ctx'=8,'head'=4] {'head'}, use_global_device_ids=true, to_apply=%region_4.5 | all-reduce | flops 2048 | bytes 16384 | tf_op jit(solution)/shard_map/psum | solution.py:54
  418.8 7.3 %multiply_convert_fusion = bf16[4,320,2048]{2,1,0:T(8,128)(2,1)} fusion(f32[4,320,2048]{2,1,0:T(8,128)} %get-tuple-element.18, f32[4,320]{1,0:T(4,128)S(1)} %mul.103, f32[2048]{0:T(1024)S(1)} %add_rsqrt_fusion), kind=kLoop, calls=%fused_computation.24 | loop fusion | flops 7864320 | bytes 15741952 | tf_op jit(solution)/shard_map/convert_element_type | solution.py:57
  426.1 7.9 %copy.35 = bf16[2048,1280]{1,0:T(8,128)(2,1)} copy(bf16[2048,1280]{0,1:T(8,128)(2,1)} %bitcast.145) | data formatting | bytes 10485760
  434.0 1.1 dynamic-slice_bitcast_fusion
  435.0 0.7 copy.36
  435.7 0.7 copy.37
  436.4 0.7 copy.38
  (13 shorter events, 0.1 us)
Async XLA Ops:
  7.2 8.0 %copy-start.5 = (bf16[40,4,320]{2,1,0:T(4,128)(2,1)S(1)}, bf16[40,4,320]{2,1,0:T(4,128)(2,1)}, u32[]{:S(2)}) copy-start(bf16[40,4,320]{2,1,0:T(4,128)(2,1)} %param.12) | copy-start | bytes 307204
  7.2 39.1 %copy-start.6 = (bf16[40,4,320]{2,1,0:T(4,128)(2,1)S(1)}, bf16[40,4,320]{2,1,0:T(4,128)(2,1)}, u32[]{:S(2)}) copy-start(bf16[40,4,320]{2,1,0:T(4,128)(2,1)} %param.13) | copy-start | bytes 307204
  7.2 379.4 %all-reduce.2.cloned.1.call-start = ((), (), s32[]{:S(2)}) async-start(), calls=%async_computation | async-start | bytes 11796480 | tf_op jit(solution)/shard_map/psum | solution.py:39
  46.3 41.5 %slice-start = ((s8[5242880]{0:T(1024)(128)(4,1)}), s8[4194304]{0:T(1024)(128)(4,1)S(1)}, s32[]{:S(2)}) async-start(s8[5242880]{0:T(1024)(128)(4,1)} %bitcast.136), calls=%async_computation.1 | async-start | bytes 8388608
  79.7 8.1 %slice-start.1 = ((s8[5242880]{0:T(1024)(128)(4,1)}), s8[1048576]{0:T(1024)(128)(4,1)S(1)}, s32[]{:S(2)}) async-start(s8[5242880]{0:T(1024)(128)(4,1)} %bitcast.136), calls=%async_computation.2 | async-start | bytes 2097152
  93.2 8.0 %copy-start.7 = (bf16[40,4,320]{2,1,0:T(4,128)(2,1)S(1)}, bf16[40,4,320]{2,1,0:T(4,128)(2,1)}, u32[]{:S(2)}) copy-start(bf16[40,4,320]{2,1,0:T(4,128)(2,1)} %param.14) | copy-start | bytes 307204
  93.2 40.6 %copy-start.4 = (f32[2048,4]{0,1:T(4,128)S(1)}, f32[2048,4]{0,1:T(4,128)}, u32[]{:S(2)}) copy-start(f32[2048,4]{0,1:T(4,128)} %param.11) | copy-start | bytes 98308
  170.0 10.7 %copy-start.2 = (f32[320,1,4,320]{3,0,2,1:T(8,128)S(1)}, f32[320,1,4,320]{3,0,2,1:T(8,128)}, u32[]{:S(2)}) copy-start(f32[320,1,4,320]{3,0,2,1:T(8,128)} %fusion.31) | copy-start | bytes 4915204
  170.0 10.7 %copy-start.3 = (f32[320,1,4,320]{3,0,2,1:T(8,128)S(1)}, f32[320,1,4,320]{3,0,2,1:T(8,128)}, u32[]{:S(2)}) copy-start(f32[320,1,4,320]{3,0,2,1:T(8,128)} %fusion.28) | copy-start | bytes 4915204
  183.8 7.9 %copy-start.8 = (f32[1280]{0:T(1024)S(1)}, f32[1280]{0:T(1024)}, u32[]{:S(2)}) copy-start(f32[1280]{0:T(1024)} %param.15) | copy-start | bytes 15364
  386.6 4.4 copy-start
  386.6 7.0 %slice-start.2 = ((s8[5242880]{0:T(1024)(128)(4,1)}), s8[4194304]{0:T(1024)(128)(4,1)S(1)}, s32[]{:S(2)}) async-start(s8[5242880]{0:T(1024)(128)(4,1)} %bitcast.140), calls=%async_computation.3 | async-start | bytes 8388608
  391.0 2.6 slice-start.3
  392.1 1.6 copy-start.1
Sparse Core Ops, SparseCore 0:
  183.9 202.6 all-reduce.1
where the time goes:
time: 448 us; the launch traced here: 444 us
  waiting for transfers between devices  195 us (44%)
  blocking collectives  103 us (23%)
  matrix products  79.5 us (18%)
  local copies, waits for them, and re-layouts  37.4 us (8%)
  other arithmetic  14.9 us (3%)
  between operations  14.2 us (3%)
    psum x1, waiting for transfers between devices, per_device(): total = lax.psum(jnp.stack([grad_gate, grad_up, grad_down], axis=1), 'ctx')  195 us
    unnamed x36, local copies, waits for them, and re-layouts  36.2 us
    all_gather x1, blocking collectives, per_device(): lax.all_gather(w_up, 'ctx', axis=0, tiled=True)  33.4 us
    all_gather x1, blocking collectives, per_device(): lax.all_gather(w_down, 'ctx', axis=0, tiled=True)  32.6 us
    all_gather x1, blocking collectives, per_device(): lax.all_gather(w_gate, 'ctx', axis=0, tiled=True)  31.1 us
    dot_general x1, matrix products, per_device(): jnp.einsum('thf,thd->fhd', dgate, keyh, preferred_element_type=jnp.float32)  15.3 us
    dot_general x1, matrix products, per_device(): jnp.einsum('thf,fhd->thd', mixed, new_down, preferred_element_type=jnp.fl...  13.7 us
    dot_general x1, matrix products, per_device(): jnp.einsum('thf,thd->fhd', hidden, scaled, preferred_element_type=jnp.flo...  13 us
  transfers between devices with their start and end apart: 1, of which 1 were waited for; matrix products, arithmetic and copies ran while one was open for 2% of the time, Pallas kernels for 0%

commit v1 on v0

v1 whole, which is shorter than its diff:
```python
import functools
import math

import jax
import jax.numpy as jnp
from jax import lax
from jax.experimental import pallas as pl
from jax.experimental.pallas import tpu as pltpu
from jax.sharding import PartitionSpec as P

EPS = 1e-06


def inner_size(n):
    inner = 1
    while inner * inner * 4 <= n and n % (inner * 2) == 0:
        inner *= 2
    return inner if inner > 1 or n % 2 else 2


def place(n, inner):
    me = lax.axis_index("ctx")
    return me, me // inner, lax.rem(me, inner), n // inner


def greet(z, x, outer, inner):
    barrier = pltpu.get_barrier_semaphore()
    for s in range(1, outer):
        pl.semaphore_signal(barrier, inc=1, device_id={"ctx": lax.rem(z + s, outer) * inner + x})
    for t in range(1, inner):
        pl.semaphore_signal(barrier, inc=1, device_id={"ctx": z * inner + lax.rem(x + t, inner)})
    pl.semaphore_wait(barrier, outer + inner - 2)


def spread(z, x, outer, inner, own_ref, out_ref, send_sem, recv_sem):
    me = z * inner + x
    copies = {}

    def send(src, block, device, s, t):
        copy = pltpu.make_async_remote_copy(
            src_ref=src,
            dst_ref=out_ref.at[block],
            send_sem=send_sem.at[s, t],
            recv_sem=recv_sem.at[s, t],
            device_id={"ctx": device},
        )
        copy.start()
        copies[s, t] = copy

    for s in range(1, outer):
        send(own_ref, me, lax.rem(z + s, outer) * inner + x, s, 0)
    for t in range(1, inner):
        send(own_ref, me, z * inner + lax.rem(x + t, inner), 0, t)
    for s in range(1, outer):
        copies[s, 0].wait_recv()
        block = lax.rem(z + outer - s, outer) * inner + x
        for t in range(1, inner):
            send(out_ref.at[block], block, z * inner + lax.rem(x + t, inner), s, t)
    for (s, t), copy in copies.items():
        if t:
            copy.wait_recv()
    for copy in copies.values():
        copy.wait_send()


def gather_kernel(n, inner, own_ref, out_ref, local_sem, send_sem, recv_sem):
    me, z, x, outer = place(n, inner)
    greet(z, x, outer, inner)
    keep = pltpu.make_async_copy(own_ref, out_ref.at[me], local_sem)
    keep.start()
    spread(z, x, outer, inner, own_ref, out_ref, send_sem, recv_sem)
    keep.wait()


def update_kernel(
    n, inner, grad_ref, old_ref, out_ref, near, part, far, fresh,
    local_sem, near_send, near_recv, far_send, far_recv, send_sem, recv_sem,
):
    me, z, x, outer = place(n, inner)
    greet(z, x, outer, inner)
    order = list(range(1, outer)) + [0]
    first = {}
    for s in order:
        row = lax.rem(z + s, outer) * inner
        for t in range(1, inner):
            column = lax.rem(x + t, inner)
            copy = pltpu.make_async_remote_copy(
                src_ref=grad_ref.at[row + column],
                dst_ref=near.at[s, t - 1],
                send_sem=near_send.at[s, t],
                recv_sem=near_recv.at[s, t],
                device_id={"ctx": z * inner + column},
            )
            copy.start()
            first[s, t] = copy
    second = {}
    total = None
    for s in order:
        row = lax.rem(z + s, outer) * inner
        total = grad_ref[row + x].astype(jnp.float32)
        for t in range(1, inner):
            first[s, t].wait_recv()
            total = total + near[s, t - 1].astype(jnp.float32)
        if s:
            part[s] = total.astype(part.dtype)
            copy = pltpu.make_async_remote_copy(
                src_ref=part.at[s],
                dst_ref=far.at[s],
                send_sem=far_send.at[s],
                recv_sem=far_recv.at[s],
                device_id={"ctx": row + x},
            )
            copy.start()
            second[s] = copy
    for s, copy in second.items():
        copy.wait_recv()
        total = total + far[s].astype(jnp.float32)
    old = old_ref[...].astype(jnp.float32)
    updated = old + total
    old_sq = jnp.sum(old * old, axis=1, keepdims=True)
    new_sq = jnp.sum(updated * updated, axis=1, keepdims=True)
    fresh[...] = (updated * (jnp.sqrt(old_sq) * lax.rsqrt(new_sq + EPS))).astype(fresh.dtype)
    keep = pltpu.make_async_copy(fresh, out_ref.at[me], local_sem)
    keep.start()
    keep.wait()
    spread(z, x, outer, inner, out_ref.at[me], out_ref, send_sem, recv_sem)
    for copy in first.values():
        copy.wait_send()
    for copy in second.values():
        copy.wait_send()


def vmem(count):
    return [pl.BlockSpec(memory_space=pltpu.VMEM)] * count


def gather(own, n):
    inner = inner_size(n)
    outer = n // inner
    return pl.pallas_call(
        functools.partial(gather_kernel, n, inner),
        out_shape=jax.ShapeDtypeStruct((n,) + own.shape, own.dtype),
        in_specs=vmem(1),
        out_specs=vmem(1)[0],
        scratch_shapes=[pltpu.SemaphoreType.DMA]
        + [pltpu.SemaphoreType.DMA((outer, inner))] * 2,
        compiler_params=pltpu.CompilerParams(collective_id=0, has_side_effects=True),
        name="gather_weights",
    )(own)


def update(grads, old, n):
    inner = inner_size(n)
    outer = n // inner
    block = grads.shape[1:]
    return pl.pallas_call(
        functools.partial(update_kernel, n, inner),
        out_shape=jax.ShapeDtypeStruct(grads.shape, grads.dtype),
        in_specs=vmem(2),
        out_specs=vmem(1)[0],
        scratch_shapes=[
            pltpu.VMEM((outer, max(inner - 1, 1)) + block, grads.dtype),
            pltpu.VMEM((outer,) + block, grads.dtype),
            pltpu.VMEM((outer,) + block, grads.dtype),
            pltpu.VMEM(block, grads.dtype),
            pltpu.SemaphoreType.DMA,
        ]
        + [pltpu.SemaphoreType.DMA((outer, inner))] * 2
        + [pltpu.SemaphoreType.DMA((outer,))] * 2
        + [pltpu.SemaphoreType.DMA((outer, inner))] * 2,
        compiler_params=pltpu.CompilerParams(collective_id=1, has_side_effects=True),
        name="update_weights",
    )(grads, old)


def dot(a, b, left, right):
    return lax.dot_general(a, b, (((left,), (right,)), ((), ())), preferred_element_type=jnp.float32)


def grads_kernel(key_ref, value_ref, rate_ref, weight_ref, out_ref, acc):
    step = pl.program_id(0)

    @pl.when(step == 0)
    def _():
        acc[...] = jnp.zeros_like(acc)

    heads, width = weight_ref.shape[1:3]
    for h in range(heads):
        columns = slice(h * width, (h + 1) * width)
        key = key_ref[:, columns]
        gpre = dot(key, weight_ref[0, h], 1, 0)
        upre = dot(key, weight_ref[1, h], 1, 0)
        scaled = (value_ref[:, columns].astype(jnp.float32) * rate_ref[:, h : h + 1]).astype(jnp.bfloat16)
        back = dot(scaled, weight_ref[2, h], 1, 0)
        sig = jax.nn.sigmoid(gpre)
        act = gpre * sig
        slope = sig * (1.0 + gpre * (1.0 - sig))
        acc[0, h] += dot(key, (back * upre * slope).astype(jnp.bfloat16), 0, 0)
        acc[1, h] += dot(key, (back * act).astype(jnp.bfloat16), 0, 0)
        acc[2, h] += dot(scaled, (act * upre).astype(jnp.bfloat16), 0, 0)

    @pl.when(step == pl.num_programs(0) - 1)
    def _():
        out_ref[...] = acc[...].astype(out_ref.dtype)


def apply_kernel(query_ref, weight_ref, out_ref, square_ref):
    heads, width = weight_ref.shape[1:3]
    squares = None
    for h in range(heads):
        columns = slice(h * width, (h + 1) * width)
        query = query_ref[:, columns]
        gate = dot(query, weight_ref[0, h], 1, 0)
        up = dot(query, weight_ref[1, h], 1, 0)
        mixed = (jax.nn.silu(gate) * up).astype(jnp.bfloat16)
        out = dot(mixed, weight_ref[2, h], 1, 1)
        part = jnp.sum(out * out, axis=1, keepdims=True)
        squares = part if squares is None else squares + part
        out_ref[:, columns] = out.astype(out_ref.dtype)
    square_ref[...] = squares


def tile(rows, width):
    return pl.BlockSpec((rows, width), lambda i: (i, 0))


def fixed(shape):
    return pl.BlockSpec(shape, lambda i: (0,) * len(shape))


def token_grads(keys, values, rates, weights):
    rows, width = keys.shape
    step = math.gcd(rows, 512)
    return pl.pallas_call(
        grads_kernel,
        grid=(rows // step,),
        out_shape=jax.ShapeDtypeStruct(weights.shape, jnp.bfloat16),
        in_specs=[tile(step, width), tile(step, width), tile(step, rates.shape[1]), fixed(weights.shape)],
        out_specs=fixed(weights.shape),
        scratch_shapes=[pltpu.VMEM(weights.shape, jnp.float32)],
        name="token_grads",
    )(keys, values, rates, weights)


def apply(queries, weights):
    rows, width = queries.shape
    step = math.gcd(rows, 512)
    return pl.pallas_call(
        apply_kernel,
        grid=(rows // step,),
        out_shape=(
            jax.ShapeDtypeStruct((rows, width), jnp.bfloat16),
            jax.ShapeDtypeStruct((rows, 1), jnp.float32),
        ),
        in_specs=[tile(step, width), fixed(weights.shape)],
        out_specs=(tile(step, width), tile(step, 1)),
        name="apply_weights",
    )(queries, weights)


def per_device(n, width_all, keys, values, queries, rates, w_gate, w_up, w_down, gain):
    rows = keys.shape[0]
    units, heads, width = w_gate.shape
    f32 = jnp.float32
    own = jnp.stack([w_gate, w_up, w_down]).transpose(0, 2, 1, 3)
    own = own.reshape(3 * heads, units, width)
    full = gather(own, n).transpose(1, 3, 0, 2)
    full = full.reshape(3, heads, width, n * units)
    grads = token_grads(keys, values, rates, full)
    block = (n, 3 * heads * width // n, n * units)
    old = lax.dynamic_index_in_dim(full.reshape(block), lax.axis_index("ctx"), 0, keepdims=False)
    fresh = update(grads.reshape(block), old, n).reshape(full.shape)
    mine = lax.dynamic_slice_in_dim(fresh, lax.axis_index("ctx") * units, units, 3)
    mine = mine.transpose(0, 3, 1, 2)
    outs, squares = apply(queries, fresh)
    squares = lax.psum(squares.reshape(rows), "head")
    scale = lax.rsqrt(squares / width_all + EPS)
    output = (outs.astype(f32) * scale[:, None] * gain[None]).astype(jnp.bfloat16)
    return (output, mine[0], mine[1], mine[2])


def solution(mesh):
    weight = P("ctx", "head", None)
    token = P("ctx", "head")

    def whole(keys, *rest):
        body = functools.partial(per_device, mesh.shape["ctx"], keys.shape[1])
        return jax.shard_map(
            body,
            mesh=mesh,
            in_specs=(token,) * 4 + (weight,) * 3 + (P("head"),),
            out_specs=(token, weight, weight, weight),
            check_vma=False,
        )(keys, *rest)

    return whole
```

time: 448 us -> 241 us (0.54)
  Pallas kernels: 0 us -> 201 us
  waiting for transfers between devices: 195 us -> 0 us
  blocking collectives: 103 us -> 5.98 us
  matrix products: 79.5 us -> 0 us
  local copies, waits for them, and re-layouts: 37.4 us -> 23.4 us
  between operations: 14.2 us -> 0.74 us
  other arithmetic: 14.9 us -> 9 us
    pallas_call x0 -> x4, Pallas kernels: none -> 201 us  [the longest x1 106 us: update(): pl.pallas_call(functools.partial(update_kernel, n, inner), out_shape=jax....]
    psum x1 -> x0, waiting for transfers between devices: 195 us -> none  [per_device(): total = lax.psum(jnp.stack([grad_gate, grad_up, grad_down], axis=1), 'ctx')]
    all_gather x3 -> x0, blocking collectives: 97.1 us -> none  [the longest x1 33.4 us: per_device(): lax.all_gather(w_up, 'ctx', axis=0, tiled=True)]
    dot_general x8 -> x0, matrix products: 79.5 us -> none  [the longest x1 15.3 us: per_device(): jnp.einsum('thf,thd->fhd', dgate, keyh, preferred_element_type=jnp.float32)]
    unnamed x36 -> x8, local copies, waits for them, and re-layouts: 36.2 us -> 4.6 us
    transpose x0 -> x4, local copies, waits for them, and re-layouts: none -> 7.55 us  [the longest x2 4.83 us: per_device(): full = gather(own, n).transpose(1, 3, 0, 2)]
    another operation x0 -> x1, local copies, waits for them, and re-layouts: none -> 6.33 us  [per_device(): full.reshape(block)]
  transfers between devices with their start and end apart: 1 -> 0, of which waited for: 1 -> 0; matrix products, arithmetic and copies ran while one was open for 2% -> 0% of each run, Pallas kernels for 0% -> 0%
where the time goes in v1:
time: 241 us; the launch traced here: 240 us
  Pallas kernels  201 us (83%)
  local copies, waits for them, and re-layouts  23.4 us (10%)
  other arithmetic  9 us (4%)
  blocking collectives  5.98 us (2%)
    pallas_call x1, Pallas kernels, update(): pl.pallas_call(functools.partial(update_kernel, n, inner), out_shape=jax....  106 us
    pallas_call x1, Pallas kernels, gather(): pl.pallas_call(functools.partial(gather_kernel, n, inner), out_shape=jax....  46.4 us
    pallas_call x1, Pallas kernels, token_grads(): pl.pallas_call(grads_kernel, grid=(rows // step,), out_shape=jax.ShapeDty...  28.9 us
    pallas_call x1, Pallas kernels, apply(): pl.pallas_call(apply_kernel, grid=(rows // step,), out_shape=(jax.ShapeDt...  19.4 us
    another operation x1, local copies, waits for them, and re-layouts, per_device(): full.reshape(block)  6.33 us
    convert_element_type x1, other arithmetic, per_device(): (outs.astype(f32) * scale[:, None] * gain[None]).astype(jnp.bfloat16)  6.1 us
    psum x1, blocking collectives, per_device(): squares = lax.psum(squares.reshape(rows), 'head')  5.98 us
    transpose x2, local copies, waits for them, and re-layouts, per_device(): full = gather(own, n).transpose(1, 3, 0, 2)  4.83 us

profile of v1, /device:TPU:22, one launch (start us, length us, event | category | flops | bytes accessed | tf_op | source)
XLA Modules:
  0.0 240.0 jit_solution(17123676697850397283)
XLA Ops:
  0.6 1.3 maximum_bitcast_fusion
  2.0 0.8 copy.18
  2.8 2.1 copy.20.rate_ref
  4.9 46.4 %gather_weights.1 = bf16[8,12,40,320]{3,2,1,0:T(8,128)(2,1)} custom-call(bf16[12,40,320]{2,1,0:T(8,128)(2,1)} %bitcast.27), custom_call_target="tpu_custom_call" | custom-call | tf_op jit(solution)/shard_map/gather_weights/pallas_call | solution.py:140
  51.3 2.3 copy.19
  53.6 2.9 %copy.21.weight_ref = bf16[3,4,320,320]{3,2,1,0:T(8,128)(2,1)} copy(bf16[3,4,320,320]{2,3,1,0:T(8,128)(2,1)S(1)} %bitcast.26) | data formatting | bytes 4915200 | tf_op jit(solution)/shard_map/reshape | solution.py:268
  56.5 0.0 copy-start
  56.5 28.9 %token_grads.1 = bf16[3,4,320,320]{3,2,1,0:T(8,128)(2,1)} custom-call(bf16[2048,1280]{1,0:T(8,128)(2,1)} %key_ref.1, bf16[2048,1280]{1,0:T(8,128)(2,1)} %value_ref.1, f32[2048,4]{1,0:T(8,128)} %copy.20.rate_ref, bf16[3,4,320,320]{3,2,1,0:T(8,128)(2,1)} %copy.21.weight_ref), custom_call_target="tpu_custom_call" | custom-call | tf_op jit(solution)/shard_map/token_grads/pallas_call | solution.py:234
  85.4 0.0 copy-done
  85.4 2.5 %copy.22 = bf16[12,320,8,40]{1,0,3,2:T(8,128)(2,1)} copy(bf16[12,320,8,40]{1,3,0,2:T(8,128)(2,1)S(1)} %bitcast.22) | data formatting | bytes 4915200 | tf_op jit(solution)/shard_map/transpose | solution.py:267
  87.9 6.3 %reshape_reshape.3 = bf16[8,480,320]{1,0,2:T(8,128)(2,1)S(1)} reshape(bf16[12,320,8,40]{1,0,3,2:T(8,128)(2,1)} %copy.22) | data formatting | bytes 4915200 | tf_op jit(solution)/shard_map/reshape;reshape | solution.py:271
  94.3 0.7 constant_dynamic-slice_fusion
  95.0 1.3 copy.23
  96.2 106.2 %update_weights.1 = bf16[8,480,320]{2,1,0:T(8,128)(2,1)} custom-call(bf16[8,480,320]{2,1,0:T(8,128)(2,1)} %bitcast.25, bf16[480,320]{1,0:T(8,128)(2,1)} %bitcast.28), custom_call_target="tpu_custom_call" | custom-call | tf_op jit(solution)/shard_map/update_weights/pallas_call | solution.py:156
  202.4 1.9 dynamic-slice_bitcast_fusion
  204.4 0.1 slice_bitcast_fusion
  204.4 0.0 copy-start.1
  204.5 0.8 copy.26
  205.3 0.8 copy.25
  206.1 0.8 copy.24
  206.9 19.4 %apply_weights.1 = (bf16[2048,1280]{1,0:T(8,128)(2,1)}, f32[2048,1]{1,0:T(8,128)}) custom-call(bf16[2048,1280]{1,0:T(8,128)(2,1)} %query_ref.1, bf16[3,4,320,320]{3,2,1,0:T(8,128)(2,1)} %bitcast.24), custom_call_target="tpu_custom_call" | custom-call | tf_op jit(solution)/shard_map/apply_weights/pallas_call | solution.py:248
  226.3 1.6 reduce
  227.9 6.0 %psum.7 = f32[2048]{0:T(1024)S(1)} all-reduce(f32[2048]{0:T(1024)S(1)} %reduce), channel_id=1, replica_groups=mesh['ctx'=8,'head'=4] {'head'}, use_global_device_ids=true, to_apply=%region_0.1 | all-reduce | flops 2048 | bytes 16384 | tf_op jit(solution)/shard_map/psum | solution.py:276
  233.9 0.0 copy-done.1
  233.9 6.1 %multiply_convert_fusion = bf16[2048,1280]{1,0:T(8,128)(2,1)} fusion(bf16[2048,1280]{1,0:T(8,128)(2,1)} %get-tuple-element.6, f32[1280]{0:T(1024)S(1)} %copy-done.1, f32[2048]{0:T(1024)S(1)} %add_rsqrt_fusion), kind=kLoop, calls=%fused_computation | loop fusion | flops 10485760 | bytes 10499072 | tf_op jit(solution)/shard_map/convert_element_type | solution.py:278
  (1 shorter events, 0.0 us)
Async XLA Ops:
  56.5 28.9 %copy-start = (bf16[8,12,40,320]{3,2,1,0:T(8,128)(2,1)S(1)}, bf16[8,12,40,320]{3,2,1,0:T(8,128)(2,1)}, u32[]{:S(2)}) copy-start(bf16[8,12,40,320]{3,2,1,0:T(8,128)(2,1)} %gather_weights.1) | copy-start | bytes 7372804
  204.4 29.4 %copy-start.1 = (f32[1280]{0:T(1024)S(1)}, f32[1280]{0:T(1024)}, u32[]{:S(2)}) copy-start(f32[1280]{0:T(1024)} %param.15) | copy-start | bytes 15364

commit v2 on v1

--- a/solution.py
+++ b/solution.py
@@ -115,7 +115,7 @@
     for s, copy in second.items():
         copy.wait_recv()
         total = total + far[s].astype(jnp.float32)
-    old = old_ref[...].astype(jnp.float32)
+    old = old_ref[me].astype(jnp.float32)
     updated = old + total
     old_sq = jnp.sum(old * old, axis=1, keepdims=True)
     new_sq = jnp.sum(updated * updated, axis=1, keepdims=True)
@@ -268,8 +268,7 @@
     full = full.reshape(3, heads, width, n * units)
     grads = token_grads(keys, values, rates, full)
     block = (n, 3 * heads * width // n, n * units)
-    old = lax.dynamic_index_in_dim(full.reshape(block), lax.axis_index("ctx"), 0, keepdims=False)
-    fresh = update(grads.reshape(block), old, n).reshape(full.shape)
+    fresh = update(grads.reshape(block), full.reshape(block), n).reshape(full.shape)
     mine = lax.dynamic_slice_in_dim(fresh, lax.axis_index("ctx") * units, units, 3)
     mine = mine.transpose(0, 3, 1, 2)
     outs, squares = apply(queries, fresh)

time: 241 us -> 242 us (level)
    another operation x1 -> x2, local copies, waits for them, and re-layouts: 6.33 us -> 9.47 us  [per_device(): full.reshape(block)]
where the time goes in v2:
time: 242 us
  Pallas kernels  202 us (83%)
  local copies, waits for them, and re-layouts  24.5 us (10%)
  other arithmetic  9 us (4%)
  blocking collectives  5.99 us (2%)
    pallas_call x1, Pallas kernels, update(): pl.pallas_call(functools.partial(update_kernel, n, inner), out_shape=jax....  107 us
    pallas_call x1, Pallas kernels, gather(): pl.pallas_call(functools.partial(gather_kernel, n, inner), out_shape=jax....  46.4 us
    pallas_call x1, Pallas kernels, token_grads(): pl.pallas_call(grads_kernel, grid=(rows // step,), out_shape=jax.ShapeDty...  28.9 us
    pallas_call x1, Pallas kernels, apply(): pl.pallas_call(apply_kernel, grid=(rows // step,), out_shape=(jax.ShapeDt...  19.4 us
    another operation x2, local copies, waits for them, and re-layouts, per_device(): full.reshape(block)  9.47 us
    convert_element_type x1, other arithmetic, per_device(): (outs.astype(f32) * scale[:, None] * gain[None]).astype(jnp.bfloat16)  6.1 us
    psum x1, blocking collectives, per_device(): squares = lax.psum(squares.reshape(rows), 'head')  5.99 us

profile of v2, /device:TPU:22, one launch (start us, length us, event | category | flops | bytes accessed | tf_op | source)
XLA Modules:
  0.0 241.8 jit_solution(2362736661740465339)
XLA Ops:
  0.6 1.3 maximum_bitcast_fusion
  2.0 0.8 copy.19
  2.8 2.1 copy.21.rate_ref
  4.9 46.4 %gather_weights.1 = bf16[8,12,40,320]{3,2,1,0:T(8,128)(2,1)} custom-call(bf16[12,40,320]{2,1,0:T(8,128)(2,1)} %bitcast.26), custom_call_target="tpu_custom_call" | custom-call | tf_op jit(solution)/shard_map/gather_weights/pallas_call | solution.py:140
  51.3 2.3 copy.20
  53.6 2.9 %copy.22.weight_ref = bf16[3,4,320,320]{3,2,1,0:T(8,128)(2,1)} copy(bf16[3,4,320,320]{2,3,1,0:T(8,128)(2,1)S(1)} %bitcast.25) | data formatting | bytes 4915200 | tf_op jit(solution)/shard_map/reshape | solution.py:268
  56.5 0.0 copy-start
  56.5 28.9 %token_grads.1 = bf16[3,4,320,320]{3,2,1,0:T(8,128)(2,1)} custom-call(bf16[2048,1280]{1,0:T(8,128)(2,1)} %key_ref.1, bf16[2048,1280]{1,0:T(8,128)(2,1)} %value_ref.1, f32[2048,4]{1,0:T(8,128)} %copy.21.rate_ref, bf16[3,4,320,320]{3,2,1,0:T(8,128)(2,1)} %copy.22.weight_ref), custom_call_target="tpu_custom_call" | custom-call | tf_op jit(solution)/shard_map/token_grads/pallas_call | solution.py:234
  85.4 0.0 copy-done
  85.4 2.5 %copy.23 = bf16[12,320,8,40]{1,0,3,2:T(8,128)(2,1)} copy(bf16[12,320,8,40]{1,3,0,2:T(8,128)(2,1)S(1)} %bitcast.21) | data formatting | bytes 4915200 | tf_op jit(solution)/shard_map/transpose | solution.py:267
  87.9 6.3 %reshape_reshape.3 = bf16[8,480,320]{1,0,2:T(8,128)(2,1)S(1)} reshape(bf16[12,320,8,40]{1,0,3,2:T(8,128)(2,1)} %copy.23) | data formatting | bytes 4915200 | tf_op jit(solution)/shard_map/reshape;reshape | solution.py:271
  94.3 3.1 %copy.24.old_ref = bf16[8,480,320]{2,1,0:T(8,128)(2,1)} copy(bf16[8,480,320]{1,0,2:T(8,128)(2,1)S(1)} %reshape_reshape.3) | data formatting | bytes 4915200 | tf_op jit(solution)/shard_map/reshape;reshape | solution.py:271
  97.4 106.9 %update_weights.1 = bf16[8,480,320]{2,1,0:T(8,128)(2,1)} custom-call(bf16[8,480,320]{2,1,0:T(8,128)(2,1)} %bitcast.24, bf16[8,480,320]{2,1,0:T(8,128)(2,1)} %copy.24.old_ref), custom_call_target="tpu_custom_call" | custom-call | tf_op jit(solution)/shard_map/update_weights/pallas_call | solution.py:156
  204.3 1.9 dynamic-slice_bitcast_fusion
  206.2 0.1 slice_bitcast_fusion
  206.3 0.0 copy-start.1
  206.3 0.8 copy.27
  207.1 0.8 copy.26
  207.9 0.8 copy.25
  208.8 19.4 %apply_weights.1 = (bf16[2048,1280]{1,0:T(8,128)(2,1)}, f32[2048,1]{1,0:T(8,128)}) custom-call(bf16[2048,1280]{1,0:T(8,128)(2,1)} %query_ref.1, bf16[3,4,320,320]{3,2,1,0:T(8,128)(2,1)} %bitcast.23), custom_call_target="tpu_custom_call" | custom-call | tf_op jit(solution)/shard_map/apply_weights/pallas_call | solution.py:248
  228.2 1.6 reduce
  229.7 6.0 %psum.7 = f32[2048]{0:T(1024)S(1)} all-reduce(f32[2048]{0:T(1024)S(1)} %reduce), channel_id=1, replica_groups=mesh['ctx'=8,'head'=4] {'head'}, use_global_device_ids=true, to_apply=%region_0.0 | all-reduce | flops 2048 | bytes 16384 | tf_op jit(solution)/shard_map/psum | solution.py:275
  235.7 0.0 copy-done.1
  235.7 6.1 %multiply_convert_fusion = bf16[2048,1280]{1,0:T(8,128)(2,1)} fusion(bf16[2048,1280]{1,0:T(8,128)(2,1)} %get-tuple-element.6, f32[1280]{0:T(1024)S(1)} %copy-done.1, f32[2048]{0:T(1024)S(1)} %add_rsqrt_fusion), kind=kLoop, calls=%fused_computation | loop fusion | flops 10485760 | bytes 10499072 | tf_op jit(solution)/shard_map/convert_element_type | solution.py:277
  (1 shorter events, 0.0 us)
Async XLA Ops:
  56.5 28.9 %copy-start = (bf16[8,12,40,320]{3,2,1,0:T(8,128)(2,1)S(1)}, bf16[8,12,40,320]{3,2,1,0:T(8,128)(2,1)}, u32[]{:S(2)}) copy-start(bf16[8,12,40,320]{3,2,1,0:T(8,128)(2,1)} %gather_weights.1) | copy-start | bytes 7372804
  206.3 29.4 %copy-start.1 = (f32[1280]{0:T(1024)S(1)}, f32[1280]{0:T(1024)}, u32[]{:S(2)}) copy-start(f32[1280]{0:T(1024)} %param.15) | copy-start | bytes 15364
